TPU v7x, 512 devices: a whole 4x8x8 slice. The times are simulated.
512 devices in a mesh: tgt: 32 (over y, x), src: 16 (over z, core).
Axes of the slice: x: 4, y: 8, z: 8, core: 2. Of those that a mesh axis runs over, the one named last changes fastest.
Arguments:
- incident: bfloat16 [128, 8, 8192], P(None, None, 'tgt'), may hold values from -6 to 6
- past_density: bfloat16 [76, 8, 8192], P(None, None, 'src'), may hold values from -6 to 6
- kernels: bfloat16 [8, 8192, 8192], P(None, 'src', 'tgt'), may hold values from -0.03125 to 0.03125
- lag_offset: int32 [32, 16, 12], P('tgt', 'src'), may hold values from 0 to 11, each once within a row
- lag_counts: int32 [32, 16], P('tgt', 'src'), may hold values from 2 to 8, as said below
- couplings: float32 [2, 8192, 256], P(None, 'tgt'), may hold values from -0.86 to 0.01
- inverse: float32 [8192, 256], P('tgt'), may hold values from -0.02 to 1.06
Outputs:
- densities: float32 [128, 8, 8192], P(None, None, 'tgt')
Inputs may be any that keep to these rules, and one draw needn't show every extreme that they name: `lag_counts`: each tile has between 2 and 8 nonzero retarded lags; in every draw some tile has 8.
All inputs are finite; a program needn't handle non-finite values.
Results may differ from a plain program's by a relative error of at most 0.0014.
Values may be sent and summed in bfloat16 or wider, within the bound.
A program may use at most 64 MiB of HBM per device.

v0:
```python
import math

import jax
import jax.numpy as jnp
from jax import lax
from jax.sharding import PartitionSpec as P

BLOCK_STEPS = 64
BLOCKS = 2
HIST = 76
COUPLINGS = 2


precise = lax.Precision.HIGHEST


def spread(array, axis, root):
    mine = lax.axis_index(axis) == root
    return lax.psum(jnp.where(mine, array, jnp.zeros_like(array)), axis)


def far_partial(
    kernels, offsets, history, first_step, start_slot, end_slot, kernel_base, partial_sum
):
    column_size = history.shape[2]

    def add_slot(slot_index, running):
        lag_value = BLOCK_STEPS + offsets[slot_index]
        window = lax.dynamic_slice_in_dim(history, first_step - lag_value + HIST, BLOCK_STEPS, 0)
        kernel_block = lax.dynamic_index_in_dim(
            kernels, slot_index - kernel_base, 0, keepdims=False
        )
        return running + jnp.dot(
            window.reshape(-1, column_size), kernel_block, preferred_element_type=jnp.float32
        )

    return lax.fori_loop(start_slot, end_slot, add_slot, partial_sum)


def impulse_table(couplings, inverse, inner_steps):
    entries = [inverse]
    for delay_index in range(1, inner_steps):
        summed = jnp.zeros_like(inverse)
        for shift_lag in range(1, min(delay_index, COUPLINGS) + 1):
            summed = summed + jnp.dot(
                entries[delay_index - shift_lag], couplings[shift_lag - 1], precision=precise
            )
        entries.append(-jnp.dot(summed, inverse, precision=precise))
    return entries


def self_response(driving, earlier_steps, couplings, responses, inner_steps):
    row_size = driving.shape[2]
    load_count = driving.shape[1]
    grouped = driving.reshape(BLOCK_STEPS // inner_steps, inner_steps, load_count, row_size)

    def advance(earlier, driving_group):
        padded = jnp.concatenate(
            [earlier, jnp.zeros((inner_steps, load_count, row_size), jnp.float32)], 0
        )
        adjusted = driving_group
        for shift_lag in range(1, COUPLINGS + 1):
            lagged = padded[COUPLINGS - shift_lag : COUPLINGS - shift_lag + inner_steps]
            adjusted = adjusted - jnp.dot(
                lagged.reshape(-1, row_size), couplings[shift_lag - 1], precision=precise
            ).reshape(adjusted.shape)
        solved = jnp.zeros_like(adjusted)
        for delay_index in range(inner_steps):
            shifted = jnp.concatenate(
                [
                    jnp.zeros((delay_index, load_count, row_size), jnp.float32),
                    adjusted[: inner_steps - delay_index],
                ],
                0,
            )
            solved = solved + jnp.dot(
                shifted.reshape(-1, row_size), responses[delay_index], precision=precise
            ).reshape(adjusted.shape)
        return (solved[inner_steps - COUPLINGS :], solved)

    earlier_steps, solved_all = lax.scan(advance, earlier_steps, grouped)
    return (earlier_steps, solved_all.reshape(BLOCK_STEPS, load_count, row_size))


def local(incident, past_density, kernels, lag_offset, lag_counts, couplings, inverse):
    row_size = incident.shape[2]
    load_count = incident.shape[1]
    column_size = past_density.shape[2]
    ratio_groups = column_size // row_size
    source_count = lax.axis_size("src")
    repeats = max(source_count // load_count, 1)
    share = max(load_count // source_count, 1)
    target = lax.axis_index("tgt")
    source = lax.axis_index("src")
    load_start = source * share % load_count
    offsets = lag_offset[0, 0]
    own_count = lag_counts[0, 0]
    inner_steps = math.gcd(BLOCK_STEPS, 8)
    responses = impulse_table(couplings, inverse, inner_steps)
    recent_piece = lax.dynamic_slice_in_dim(
        past_density[HIST - COUPLINGS :], target * row_size - source * column_size, row_size, 2
    )
    earlier_steps = spread(recent_piece, "src", target // ratio_groups).astype(jnp.float32)
    earlier_steps = lax.dynamic_slice_in_dim(earlier_steps, load_start, share, 1)
    history = past_density
    produced = []
    for block_index in range(BLOCKS):
        first_step = block_index * BLOCK_STEPS
        partial_sum = jnp.zeros((BLOCK_STEPS * load_count, row_size), jnp.float32)
        partial_sum = far_partial(
            kernels, offsets, history, first_step, jnp.int32(0), own_count, 0, partial_sum
        )
        incident_block = incident[first_step : first_step + BLOCK_STEPS].astype(jnp.float32)
        term = jnp.tile(partial_sum.reshape(BLOCK_STEPS, load_count, row_size), (1, repeats, 1))
        far_share = lax.psum_scatter(term, "src", scatter_dimension=1, tiled=True)
        driving = lax.dynamic_slice_in_dim(incident_block, load_start, share, 1) - far_share
        earlier_steps, solved_share = self_response(
            driving, earlier_steps, couplings, responses, inner_steps
        )
        every_load = lax.all_gather(solved_share, "src", axis=1, tiled=True)
        fresh_block = every_load[:, :load_count]
        produced.append(fresh_block)
        if block_index + 1 < BLOCKS:
            rounded = fresh_block.astype(jnp.bfloat16)
            gathered = lax.all_gather(rounded, "tgt", axis=2, tiled=True)
            columns = lax.dynamic_slice_in_dim(gathered, source * column_size, column_size, 2)
            history = jnp.concatenate([history, columns], 0)
    return jnp.concatenate(produced, 0)


def solution(mesh):
    return jax.shard_map(
        local,
        mesh=mesh,
        in_specs=(
            P(None, None, "tgt"),
            P(None, None, "src"),
            P(None, "src", "tgt"),
            P("tgt", "src", None),
            P("tgt", "src"),
            P(None, "tgt", None),
            P("tgt", None),
        ),
        out_specs=P(None, None, "tgt"),
        check_vma=False,
    )
```

profile of v0, /device:TPU:1, one launch (start us, length us, event | category | flops | bytes accessed | tf_op | source)
XLA Modules:
  0.0 448.3 jit_solution(3209630210524945788)
XLA Ops:
  6.6 12.6 %while.48 = (s32[]{:T(128)}, f32[512,256]{1,0:T(8,128)S(1)}, s32[]{:T(128)}, s32[12]{0:T(128)}, bf16[76,8,512]{2,1,0:T(8,128)(2,1)}, /*index=5*/bf16[8,512,256]{...) while((s32[]{:T(128)}, f32[512,256]{1,0:T(8,128)S(1)}, ...), condition=%wide.region_2.3_spmd, body=%wide.region_1.2_spmd.sunk | while | flops 134348816 | bytes 1835278 | solution.py:37
  7.2 1.3 dynamic_slice.102
  9.1 1.4 convolution_add_fusion.36
  11.2 1.3 dynamic_slice.102
  13.1 1.4 convolution_add_fusion.36
  15.2 1.3 dynamic_slice.102
  17.1 1.4 convolution_add_fusion.36
  20.7 47.4 %psum.7 = bf16[2,8,256]{2,0,1:T(2,128)(2,1)S(1)} all-reduce(bf16[2,8,256]{2,0,1:T(2,128)(2,1)S(1)} %broadcast_select_fusion), channel_id=1, replica_groups=mesh['tgt'=32,'src'=16] {'src'}, use_global_device_ids=true, to_apply=%region_0.1 | all-reduce | flops 4096 | bytes 16384 | tf_op jit(solution)/shard_map/psum | solution.py:19
  73.5 1.6 constant_dynamic-slice_fusion.2
  78.2 26.9 %reduce-scatter.3.cloned.1.call-done = f32[64,1,256]{2,0,1:T(8,128)} async-done(((f32[64,16,256]{2,0,1:T(8,128)}), f32[64,1,256]{2,0,1:T(8,128)}) %reduce-scatter.3.cloned.1.call-update) | async-done | bytes 65552 | tf_op jit(solution)/shard_map/reduce_scatter | solution.py:115
  105.1 1.5 subtract_bitcast_fusion.1
  107.2 29.2 %while.49 = (s32[]{:T(128)}, f32[2,1,256]{2,0,1:T(2,128)S(1)}, f32[8,8,1,256]{3,1,2,0:T(8,128)}, f32[8,8,1,256]{3,1,2,0:T(8,128)}, f32[2,256,256]{2,1,0:T(8,128)...) while((s32[]{:T(128)}, f32[2,1,256]{2,0,1:T(2,128)S(1)}, ...), condition=%wide.region_5.6_spmd, body=%wide.region_4.5_spmd.sunk | while | flops 62932992 | bytes 2887829 | solution.py:81
  136.5 42.8 %all-gather.4.cloned.1.call-done = f32[64,16,256]{2,0,1:T(8,128)} async-done(((f32[64,1,256]{2,0,1:T(8,128)}), f32[64,16,256]{2,0,1:T(8,128)}) %all-gather.4.cloned.1.call-update) | async-done | bytes 1048592 | tf_op jit(solution)/shard_map/all_gather | solution.py:120
  179.3 1.8 slice.278
  181.1 103.1 %all-gather.6.cloned.1.call-done = bf16[64,8,8192]{2,0,1:T(8,128)(2,1)} async-done(((bf16[64,8,256]{2,0,1:T(8,128)(2,1)}), bf16[64,8,8192]{2,0,1:T(8,128)(2,1)}) %all-gather.6.cloned.1.call-update) | async-done | bytes 8388624 | tf_op jit(solution)/shard_map/all_gather | solution.py:125
  285.6 1.1 pad_maximum_fusion
  286.8 10.7 %while.50 = (s32[]{:T(128)}, f32[512,256]{1,0:T(8,128)S(1)}, s32[]{:T(128)}, s32[12]{0:T(128)S(1)}, bf16[140,8,512]{2,1,0:T(8,128)(2,1)}, /*index=5*/bf16[8,512,...) while((s32[]{:T(128)}, f32[512,256]{1,0:T(8,128)S(1)}, ...), condition=%wide.region_7.8_spmd, body=%wide.region_6.7_spmd.sunk | while | flops 134348816 | bytes 1835266 | solution.py:37
  288.7 1.4 convolution_add_fusion.43
  292.1 1.4 convolution_add_fusion.43
  295.4 1.4 convolution_add_fusion.43
  298.9 76.4 %reduce-scatter.5.cloned.1.call-done = f32[64,1,256]{2,0,1:T(8,128)} async-done(((f32[64,16,256]{2,0,1:T(8,128)}), f32[64,1,256]{2,0,1:T(8,128)}) %reduce-scatter.5.cloned.1.call-update) | async-done | bytes 65552 | tf_op jit(solution)/shard_map/reduce_scatter | solution.py:115
  376.2 19.0 %while.51 = (s32[]{:T(128)}, f32[2,1,256]{2,0,1:T(2,128)S(1)}, f32[8,8,1,256]{3,1,2,0:T(8,128)S(1)}, f32[8,8,1,256]{3,1,2,0:T(8,128)S(1)}, f32[2,256,256]{2,1,0:...) while((s32[]{:T(128)}, f32[2,1,256]{2,0,1:T(2,128)S(1)}, ...), condition=%wide.region_10.11_spmd, body=%wide.region_9.10_spmd.sunk | while | flops 62932992 | bytes 2887829 | solution.py:81
  395.9 43.1 %all-gather.8.cloned.1.call-done = f32[64,16,256]{2,0,1:T(8,128)} async-done(((f32[64,1,256]{2,0,1:T(8,128)}), f32[64,16,256]{2,0,1:T(8,128)}) %all-gather.8.cloned.1.call-update) | async-done | bytes 1048592 | tf_op jit(solution)/shard_map/all_gather | solution.py:120
  440.2 1.6 copy.26
  (354 shorter events, 64.8 us)
Async XLA Ops:
  6.5 98.6 %reduce-scatter.3.cloned.1.call-start = ((), (), s32[]{:S(2)}) async-start(), calls=%async_computation.2 | async-start | bytes 1114112 | tf_op jit(solution)/shard_map/reduce_scatter | solution.py:115
  19.2 1.4 copy-start.2
  19.2 48.9 %copy-start = (f32[2,256,256]{2,1,0:T(8,128)S(1)}, f32[2,256,256]{2,1,0:T(8,128)}, u32[]{:S(2)}) copy-start(f32[2,256,256]{2,1,0:T(8,128)} %param.20) | copy-start | bytes 1572868
  19.2 48.9 %copy-start.1 = (f32[256,256]{1,0:T(8,128)S(1)}, f32[256,256]{1,0:T(8,128)}, u32[]{:S(2)}) copy-start(f32[256,256]{1,0:T(8,128)} %param.21) | copy-start | bytes 786436
  20.5 158.8 %all-gather.4.cloned.1.call-start = ((), (), s32[]{:S(2)}) async-start(), calls=%async_computation.3 | async-start | bytes 1114112 | tf_op jit(solution)/shard_map/all_gather | solution.py:120
  70.8 2.0 copy-start.3
  136.5 147.8 %all-gather.6.cloned.1.call-start = ((), (), s32[]{:S(2)}) async-start(), calls=%async_computation.4 | async-start | bytes 8650752 | tf_op jit(solution)/shard_map/all_gather | solution.py:125
  181.1 194.3 %reduce-scatter.5.cloned.1.call-start = ((), (), s32[]{:S(2)}) async-start(), calls=%async_computation.5 | async-start | bytes 1114112 | tf_op jit(solution)/shard_map/reduce_scatter | solution.py:115
  285.3 1.5 copy-start.5
  298.8 140.2 %all-gather.8.cloned.1.call-start = ((), (), s32[]{:S(2)}) async-start(), calls=%async_computation.6 | async-start | bytes 1114112 | tf_op jit(solution)/shard_map/all_gather | solution.py:120
  395.2 0.6 copy-start.4
  395.2 44.8 %slice-start = ((f32[64,16,256]{2,0,1:T(8,128)}), f32[64,8,256]{2,0,1:T(8,128)S(1)}, s32[]{:S(2)}) async-start(f32[64,16,256]{2,0,1:T(8,128)} %all-gather.4.cloned.1.call-done), calls=%async_computation.7 | async-start | bytes 1048576 | tf_op jit(solution)/shard_map/slice | solution.py:121
Sparse Core Ops, SparseCore 0:
  20.6 84.4 reduce-scatter.2
  136.6 42.6 all-gather.3
  182.3 101.8 all-gather.5
  298.9 76.4 reduce-scatter.4
  396.0 42.8 all-gather.7
where the time goes:
time: 450 us; the launch traced here: 448 us
  waiting for transfers between devices  292 us (65%)
  matrix products  62 us (14%)
  blocking collectives  47.4 us (11%)
  local copies, waits for them, and re-layouts  18.8 us (4%)
  between operations  13.6 us (3%)
  loops' own time  10.4 us (2%)
    reduce_scatter x2, waiting for transfers between devices, local(): far_share = lax.psum_scatter(term, 'src', scatter_dimension=1, tiled=True)  103 us
    all_gather x1, waiting for transfers between devices, local(): gathered = lax.all_gather(rounded, 'tgt', axis=2, tiled=True)  103 us
    all_gather x2, waiting for transfers between devices, local(): every_load = lax.all_gather(solved_share, 'src', axis=1, tiled=True)  85.8 us
    psum x1, blocking collectives, spread(): return lax.psum(jnp.where(mine, array, jnp.zeros_like(array)), axis)  47.4 us
    dot_general x128, matrix products, advance(): jnp.dot(shifted.reshape(-1, row_size), responses[delay_index], precision=...  33.7 us
    dot_general x32, matrix products, advance(): jnp.dot(lagged.reshape(-1, row_size), couplings[shift_lag - 1], precision...  12.2 us
    another operation x2, loops' own time, far_partial(): return lax.fori_loop(start_slot, end_slot, add_slot, partial_sum)  9.23 us
  transfers between devices with their start and end apart: 5, of which 5 were waited for; matrix products, arithmetic and copies ran while one was open for 2% of the time, Pallas kernels for 0%

commit v1 on v0

v1 whole, which is shorter than its diff:
```python
import functools

import jax
import jax.numpy as jnp
from jax import lax
from jax.experimental import pallas as pl
from jax.experimental.pallas import tpu as pltpu
from jax.sharding import PartitionSpec as P

BLOCKS = 2
LANE = 128
X = 4
MESH = pl.DeviceIdType.MESH
F32 = jnp.float32
BF16 = jnp.bfloat16

C1, C2, INV, A1, A2, Q1, Q2, Q3, D2 = range(9)


def split(value):
    hi = value.astype(BF16)
    return hi, (value - hi.astype(F32)).astype(BF16)


def dot(a, b):
    return jnp.dot(a, b, preferred_element_type=F32)


def dot3(a, b):
    return dot(a[0], b[0]) + dot(a[1], b[0]) + dot(a[0], b[1])


def kernel(
    off_ref, cnt_ref, inc_hbm, past_hbm, ker_hbm, cpl_hbm, inv_hbm, out_hbm,
    inc_v, past_v, ker_v, cpl_v, inv_v, hist, part, abuf, ssum, bsend, brecv,
    tab_hi, tab_lo, mat_hi, mat_lo, pads, shifts, drive, state, tsend, pieces, outbuf, obuf,
    load_sem, a_send, a_recv, b_send, b_recv, st_send, st_recv, t_send, p_recv,
    y_send, x_send, o_send, o_recv, f_send, out_sem,
    *, nz,
):
    slots, cols, rows = ker_v.shape
    history, loads, _ = past_v.shape
    block = inc_v.shape[0] // BLOCKS
    half = block // 2
    lead = history - block
    hrows = half * loads
    ny = nz
    t = lax.axis_index("tgt")
    s = lax.axis_index("src")
    y, x = t // X, t % X
    z, c = s // 2, s % 2
    oc = 1 - c
    member = c == x // 2
    xs_own = x % 2

    def at(y_, x_, z_, c_):
        return {"tgt": y_ * X + x_, "src": z_ * 2 + c_}

    def remote(src, dst, ssem, rsem, dev):
        return pltpu.make_async_remote_copy(
            src_ref=src, dst_ref=dst, send_sem=ssem, recv_sem=rsem,
            device_id=dev, device_id_type=MESH)

    partner = at(y, x, z, oc)

    barrier = pltpu.get_barrier_semaphore()

    def greet(dev):
        pl.semaphore_signal(barrier, inc=1, device_id=dev, device_id_type=MESH)

    for dz in range(1, nz):
        greet(at(y, x, (z + dz) % nz, c))
    greet(partner)

    @pl.when(member)
    def _():
        for core in range(2):
            greet(at(z, x, (2 * z + nz // 2 + nz - y) % nz, core))
        for dy in range(1, ny):
            greet(at((y + dy) % ny, x, z, c))

    for xs in range(2):
        @pl.when(2 * c + xs != x)
        def _():
            greet(at(y, 2 * c + xs, z, c))

    loads_list = [
        pltpu.make_async_copy(past_hbm, past_v, load_sem.at[0]),
        pltpu.make_async_copy(cpl_hbm, cpl_v, load_sem.at[1]),
        pltpu.make_async_copy(inv_hbm, inv_v, load_sem.at[2]),
        pltpu.make_async_copy(inc_hbm, inc_v, load_sem.at[3]),
    ]
    ker_loads = [
        pltpu.make_async_copy(ker_hbm.at[q], ker_v.at[q], load_sem.at[4 + q]) for q in range(slots)
    ]
    loads_list[0].start()
    for copy in ker_loads:
        copy.start()
    for copy in loads_list[1:]:
        copy.start()

    for blk in range(BLOCKS):
        hist[blk, :, history * loads:, :] = jnp.zeros((cols // LANE, block * loads, LANE), F32)
    pads[:, :half, :] = jnp.zeros((2, half, rows), F32)

    @pl.when(c == 0)
    def _():
        state[0] = jnp.zeros_like(state[0])

    tab_hi[0:rows, :] = jnp.zeros((rows, rows), BF16)
    tab_lo[0:rows, :] = jnp.zeros((rows, rows), BF16)

    loads_list[0].wait()
    for part_at in range(cols // LANE):
        lanes = slice(part_at * LANE, (part_at + 1) * LANE)
        earlier_steps = past_v[:, :, lanes].astype(F32).reshape(history * loads, LANE)
        hist[0, part_at, 0:history * loads, :] = earlier_steps
        hist[1, part_at, 0:lead * loads, :] = earlier_steps[block * loads:]

    def put(place, value):
        hi, lo = split(value)
        mat_hi[place] = hi
        mat_lo[place] = lo

    def mat(place):
        return mat_hi[place], mat_lo[place]

    loads_list[1].wait()
    loads_list[2].wait()
    put(C1, cpl_v[0])
    put(C2, cpl_v[1])
    put(INV, inv_v[...])
    for copy in ker_loads:
        copy.wait()

    def far(blk, h):
        total = None
        for q in range(slots):
            used = lax.max(lax.min(cnt_ref[0] - q, jnp.int32(1)), jnp.int32(0))
            first = history + used * (lead - history - off_ref[q]) + h * half
            place = pl.ds(first * loads, hrows)
            window = jnp.concatenate(
                [hist[blk, k, place, :].astype(BF16) for k in range(cols // LANE)], 1)
            term = dot(window, ker_v[q])
            total = term if total is None else total + term
        part[blk, pl.ds(pl.multiple_of(h * hrows, hrows), hrows), :] = total

    held = jnp.logical_and(z == y, member)

    def earlier(step):
        both = past_v[step].astype(F32)
        return jnp.where(xs_own == 0, both[:, :rows], both[:, rows:])

    last, before = split(earlier(history - 1)), split(earlier(history - 2))
    first_term = dot3(last, mat(C1)) + dot3(before, mat(C2))
    second_term = dot3(last, mat(C2))

    def far_first(h):
        far(0, h)
        keep = jnp.where(jnp.logical_and(held, h == 0), 1.0, 0.0).astype(F32)
        base = pl.multiple_of(h * hrows, hrows)
        part[0, pl.ds(base, loads), :] = part[0, pl.ds(base, loads), :] + keep * first_term
        base2 = pl.multiple_of(h * hrows + loads, loads)
        part[0, pl.ds(base2, loads), :] = part[0, pl.ds(base2, loads), :] + keep * second_term

    far_first(oc)

    @pl.when(member)
    def _():
        pl.semaphore_wait(barrier, nz + 1 + ny - 1 + X - 1)

    @pl.when(jnp.logical_not(member))
    def _():
        pl.semaphore_wait(barrier, nz + 1)

    def pair_copy(blk):
        other = pl.ds(pl.multiple_of(oc * hrows, hrows), hrows)
        return remote(part.at[blk, other], abuf.at[blk], a_send.at[blk], a_recv.at[blk], partner)

    pair_copy(0).start()
    far_first(c)

    def ring_send(blk, dz):
        there = (z + dz) % nz
        return remote(bsend.at[blk, there], brecv.at[blk, z], b_send.at[blk, dz], b_recv.at[blk, z],
                      at(y, x, there, c))

    def ring_arrival(blk, dz):
        there = (z + nz - dz) % nz
        return remote(bsend.at[blk, there], brecv.at[blk, there], b_send.at[blk, dz],
                      b_recv.at[blk, there], at(y, x, there, c))

    far_order = sorted(range(1, nz), key=lambda dz: -min(dz, nz - dz))
    near_order = sorted(range(1, nz), key=lambda dz: min(dz, nz - dz))

    def reduce_start(blk):
        pair_copy(blk).wait_recv()
        mine = pl.ds(pl.multiple_of(c * hrows, hrows), hrows)
        both = part[blk, mine, :] + abuf[blk]
        for k in range(rows // LANE):
            lanes = slice(k * LANE, (k + 1) * LANE)
            ssum[k] = both[:, lanes]
            for load in range(loads):
                bsend[blk, load, :, lanes] = ssum[k, pl.ds(load, half, stride=loads), :]
        for dz in far_order:
            ring_send(blk, dz).start()

    def reduce_finish(blk):
        total = bsend[blk, z]
        for dz in near_order:
            ring_arrival(blk, dz).wait_recv()
            total = total + brecv[blk, (z + nz - dz) % nz]
        return total

    loads_list[3].wait()
    row_at = lax.broadcasted_iota(jnp.int32, (half, hrows), 0) * loads + z
    pick = (row_at == lax.broadcasted_iota(jnp.int32, (half, hrows), 1)).astype(BF16)
    for blk in range(BLOCKS):
        steps = inc_v[pl.ds(blk * block + c * half, half)].astype(F32).reshape(hrows, rows)
        drive[blk] = dot(pick, steps.astype(BF16))

    reduce_start(0)

    def table_put(first, count, value):
        hi, lo = split(value)
        place = pl.ds(pl.multiple_of((first + 1) * rows, rows), count * rows)
        tab_hi[place, :] = hi
        tab_lo[place, :] = lo

    put(A1, -dot3(mat(C1), mat(INV)))
    put(A2, -dot3(mat(C2), mat(INV)))
    put(Q1, dot3(mat(A1), mat(A1)) + (mat_hi[A2].astype(F32) + mat_lo[A2].astype(F32)))
    put(Q2, dot3(mat(Q1), mat(A1)) + dot3(mat(A1), mat(A2)))
    put(Q3, dot3(mat(Q2), mat(A1)) + dot3(mat(Q1), mat(A2)))
    put(D2, dot3(mat(A2), mat(Q2)))
    table_put(0, 1, inv_v[...])
    table_put(1, 1, dot3(mat(INV), mat(A1)))
    table_put(2, 1, dot3(mat(INV), mat(Q1)))
    table_put(3, 1, dot3(mat(INV), mat(Q2)))

    def four_more(step, carry):
        one = pl.ds(pl.multiple_of((4 * step - 3) * rows, rows), 4 * rows)
        two = pl.ds(pl.multiple_of((4 * step - 4) * rows, rows), 4 * rows)
        value = dot3((tab_hi[one, :], tab_lo[one, :]), mat(Q3))
        value = value + dot3((tab_hi[two, :], tab_lo[two, :]), mat(D2))
        table_put(4 * step, 4, value)
        return carry

    lax.fori_loop(1, half // 4, four_more, 0)

    def state_copy(which):
        blk = which // 2
        held_by = which % 2
        return remote(outbuf.at[blk, c, z, pl.ds(half - 8, 8)], state.at[(which + 1) // 2],
                      st_send.at[which], st_recv.at[which], partner), held_by

    def state_start(which):
        copy, held_by = state_copy(which)

        @pl.when(c == held_by)
        def _():
            copy.start()

    def state_wait(which):
        copy, held_by = state_copy(which)

        @pl.when(c != held_by)
        def _():
            copy.wait_recv()

    def state_sent(which):
        copy, held_by = state_copy(which)

        @pl.when(c == held_by)
        def _():
            copy.wait_send()

    def solve(blk):
        drive[blk] = drive[blk] - reduce_finish(blk)
        if blk == 0:
            state_wait(0)
        else:
            state_wait(1)
            state_wait(2)
        from_state = split(state[blk])
        by_one, by_two = dot3(from_state, mat(C1)), dot3(from_state, mat(C2))
        row = lax.broadcasted_iota(jnp.int32, by_one.shape, 0)
        change = jnp.where(row == 0, pltpu.roll(by_one, 1, 0), 0.0)
        change = change + jnp.where(row < 2, pltpu.roll(by_two, 2, 0), 0.0)
        drive[blk, 0:8] = drive[blk, 0:8] - change
        hi, lo = split(drive[blk])
        pads[0, half:, :] = hi.astype(F32)
        pads[1, half:, :] = lo.astype(F32)
        for k in range(half):
            there = slice(k * rows, (k + 1) * rows)
            shifts[0:half, there] = pads[0, half - k:2 * half - k, :].astype(BF16)
            shifts[half:, there] = pads[1, half - k:2 * half - k, :].astype(BF16)
        both = dot(shifts[...], tab_hi[rows:, :])
        outbuf[blk, c, z] = both[:half] + both[half:] + dot(shifts[0:half, :], tab_lo[rows:, :])

    solve(0)
    state_start(0)
    state_start(1)

    def turn_copy():
        dst = pieces.at[c, xs_own, z]
        return remote(tsend, dst, t_send.at[0], p_recv.at[c, xs_own, z],
                      at((2 * y + nz // 2 + nz - z) % ny, x, y, x // 2))

    tsend[...] = outbuf[0, c, z].astype(BF16)
    turn_copy().start()

    def load_of(y_):
        return (2 * z + nz // 2 + nz - y_) % nz

    def piece(h, xs, load, ssem, dev):
        ref = pieces.at[h, xs, load]
        return remote(ref, ref, ssem, p_recv.at[h, xs, load], dev)

    def along_y(h, dy):
        return piece(h, xs_own, load_of(y), y_send.at[h, dy], at((y + dy) % ny, x, z, c))

    def along_x(h, dy, dx):
        load = load_of((y + ny - dy) % ny)
        return piece(h, xs_own, load, x_send.at[h, dy, dx], at(y, (x + dx) % X, z, c))

    def hand_on(h):
        @pl.when(member)
        def _():
            piece(h, xs_own, load_of(y), y_send.at[h, 0], partner).wait_recv()
            for dy in far_order:
                along_y(h, dy).start()
            for dx in (2, 1, 3):
                along_x(h, 0, dx).start()
            for dy in near_order:
                load = load_of((y + ny - dy) % ny)
                piece(h, xs_own, load, y_send.at[h, dy], partner).wait_recv()
                for dx in (2, 1, 3):
                    along_x(h, dy, dx).start()

    def take_in(h):
        for xs in range(2):
            @pl.when(2 * c + xs != x)
            def _():
                for load in range(loads):
                    piece(h, xs, load, x_send.at[h, 0, 0], partner).wait_recv()
        for xs in range(2):
            for load in range(loads):
                to = pl.ds((lead + h * half) * loads + load, half, stride=loads)
                for k in range(rows // LANE):
                    part_of = pieces[h, xs, load, :, k * LANE:(k + 1) * LANE]
                    hist[1, xs * (rows // LANE) + k, to, :] = part_of.astype(F32)

    def own_copy(blk, dz):
        ref = outbuf.at[blk, c, z]
        there = (z + dz) % nz
        return remote(ref, ref, o_send.at[blk, dz], o_recv.at[blk, c, z], at(y, x, there, c))

    def cross_copy(blk, h, from_z, dz):
        ref = outbuf.at[blk, h, from_z]
        return remote(ref, ref, f_send.at[blk, dz], o_recv.at[blk, h, from_z], partner)

    def spread_start(blk):
        for dz in far_order:
            own_copy(blk, dz).start()
        cross_copy(blk, c, z, 0).start()

    def spread_cross(blk):
        for dz in near_order:
            from_z = (z + nz - dz) % nz
            cross_copy(blk, c, from_z, dz).wait_recv()
            cross_copy(blk, c, from_z, dz).start()

    def spread_finish(blk):
        for dz in range(nz):
            cross_copy(blk, oc, (z + nz - dz) % nz, dz).wait_recv()

    def out_copy(blk, k):
        place = pl.ds(blk * block * loads, block * loads)
        return pltpu.make_async_copy(
            obuf.at[k, place], out_hbm.at[place, pl.ds(k * LANE, LANE)], out_sem.at[blk, k])

    def interleave(blk):
        for k in range(rows // LANE):
            for h in range(2):
                for load in range(loads):
                    to = pl.ds((blk * block + h * half) * loads + load, half, stride=loads)
                    obuf[k, to, :] = outbuf[blk, h, load, :, k * LANE:(k + 1) * LANE]
            out_copy(blk, k).start()

    hand_on(0)
    hand_on(1)
    spread_start(0)
    take_in(0)
    far(1, 0)

    @pl.when(c == 1)
    def _():
        pair_copy(1).start()

    @pl.when(c == 0)
    def _():
        reduce_start(1)

    take_in(1)
    far(1, 1)

    @pl.when(c == 0)
    def _():
        pair_copy(1).start()

    @pl.when(c == 1)
    def _():
        reduce_start(1)

    spread_cross(0)
    spread_finish(0)
    interleave(0)

    solve(1)
    state_start(2)
    spread_start(1)
    spread_cross(1)
    spread_finish(1)
    interleave(1)

    for blk in range(BLOCKS):
        pair_copy(blk).wait_send()
        for dz in range(1, nz):
            ring_send(blk, dz).wait_send()
            own_copy(blk, dz).wait_send()
        for dz in range(nz):
            cross_copy(blk, c, (z + nz - dz) % nz, dz).wait_send()
        for k in range(rows // LANE):
            out_copy(blk, k).wait()
    for which in range(3):
        state_sent(which)
    turn_copy().wait_send()

    @pl.when(member)
    def _():
        for h in range(2):
            for dy in range(1, ny):
                along_y(h, dy).wait_send()
            for dy in range(ny):
                for dx in range(1, X):
                    along_x(h, dy, dx).wait_send()


def local(nz, incident, past_density, kernels, lag_offset, lag_counts, couplings, inverse):
    steps, loads, rows = incident.shape
    history, _, cols = past_density.shape
    slots = kernels.shape[0]
    block = steps // BLOCKS
    half = block // 2
    hrows = half * loads
    vmem = pltpu.VMEM
    dma = pltpu.SemaphoreType.DMA
    out = pl.pallas_call(
        functools.partial(kernel, nz=nz),
        out_shape=jax.ShapeDtypeStruct((steps * loads, rows), F32),
        in_specs=[pl.BlockSpec(memory_space=pltpu.SMEM)] * 2
        + [pl.BlockSpec(memory_space=pl.ANY)] * 5,
        out_specs=pl.BlockSpec(memory_space=pl.ANY),
        scratch_shapes=[
            vmem((steps, loads, rows), BF16),
            vmem((history, loads, cols), BF16),
            vmem((slots, cols, rows), BF16),
            vmem((2, rows, rows), F32),
            vmem((rows, rows), F32),
            vmem((BLOCKS, cols // LANE, (history + block) * loads, LANE), F32),
            vmem((BLOCKS, block * loads, rows), F32),
            vmem((BLOCKS, hrows, rows), F32),
            vmem((rows // LANE, hrows, LANE), F32),
            vmem((BLOCKS, nz, half, rows), F32),
            vmem((BLOCKS, nz, half, rows), F32),
            vmem(((half + 1) * rows, rows), BF16),
            vmem(((half + 1) * rows, rows), BF16),
            vmem((9, rows, rows), BF16),
            vmem((9, rows, rows), BF16),
            vmem((2, 2 * half, rows), F32),
            vmem((2 * half, half * rows), BF16),
            vmem((BLOCKS, half, rows), F32),
            vmem((2, 8, rows), F32),
            vmem((half, rows), BF16),
            vmem((2, 2, loads, half, rows), BF16),
            vmem((BLOCKS, 2, nz, half, rows), F32),
            vmem((rows // LANE, steps * loads, LANE), F32),
            dma((4 + slots,)),
            dma((BLOCKS,)),
            dma((BLOCKS,)),
            dma((BLOCKS, nz)),
            dma((BLOCKS, nz)),
            dma((3,)),
            dma((3,)),
            dma((1,)),
            dma((2, 2, loads)),
            dma((2, nz)),
            dma((2, nz, X)),
            dma((BLOCKS, nz)),
            dma((BLOCKS, 2, nz)),
            dma((BLOCKS, nz)),
            dma((BLOCKS, rows // LANE)),
        ],
        compiler_params=pltpu.CompilerParams(
            collective_id=0, has_side_effects=True, vmem_limit_bytes=60 * 1024 * 1024),
    )(
        lag_offset.reshape(-1), lag_counts.reshape(-1),
        incident, past_density, kernels, couplings, inverse,
    )
    return out.reshape(steps, loads, rows)


def solution(mesh):
    return jax.shard_map(
        functools.partial(local, mesh.shape["src"] // 2),
        mesh=mesh,
        in_specs=(
            P(None, None, "tgt"),
            P(None, None, "src"),
            P(None, "src", "tgt"),
            P("tgt", "src", None),
            P("tgt", "src"),
            P(None, "tgt", None),
            P("tgt", None),
        ),
        out_specs=P(None, None, "tgt"),
        check_vma=False,
    )
```

time: 450 us -> 69.1 us (0.15)
  waiting for transfers between devices: 292 us -> 0 us
  Pallas kernels: 0 us -> 66 us
  matrix products: 62 us -> 0 us
  blocking collectives: 47.4 us -> 0 us
  local copies, waits for them, and re-layouts: 18.8 us -> 2.26 us
  between operations: 13.6 us -> 0.66 us
  loops' own time: 10.4 us -> 0 us
    all_gather x3 -> x0, waiting for transfers between devices: 189 us -> none  [the longest x1 103 us: local(): gathered = lax.all_gather(rounded, 'tgt', axis=2, tiled=True)]
    reduce_scatter x2 -> x0, waiting for transfers between devices: 103 us -> none  [local(): far_share = lax.psum_scatter(term, 'src', scatter_dimension=1, tiled=True)]
    pallas_call x0 -> x1, Pallas kernels: none -> 66 us  [local(): pl.pallas_call(functools.partial(kernel, nz=nz), out_shape=jax.ShapeDtype...]
    dot_general x186 -> x0, matrix products: 62 us -> none  [the longest x128 33.7 us: advance(): jnp.dot(shifted.reshape(-1, row_size), responses[delay_index], precision=...]
    psum x1 -> x0, blocking collectives: 47.4 us -> none  [spread(): return lax.psum(jnp.where(mine, array, jnp.zeros_like(array)), axis)]
    another operation x4 -> x0, loops' own time: 10.4 us -> none  [the longest x2 9.23 us: far_partial(): return lax.fori_loop(start_slot, end_slot, add_slot, partial_sum)]
    dynamic_slice x11 -> x0, local copies, waits for them, and re-layouts: 8.63 us -> none  [the longest x6 5.53 us: add_slot(): lag_value = BLOCK_STEPS + offsets[slot_index]]
    slice x118 -> x0, local copies, waits for them, and re-layouts: 4.61 us -> none  [the longest x4 2.86 us: local(): fresh_block = every_load[:, :load_count]]
  transfers between devices with their start and end apart: 5 -> 0, of which waited for: 5 -> 0; matrix products, arithmetic and copies ran while one was open for 2% -> 0% of each run, Pallas kernels for 0% -> 0%
where the time goes in v1:
time: 69.1 us; the launch traced here: 68.9 us
  Pallas kernels  66 us (96%)
  local copies, waits for them, and re-layouts  2.26 us (3%)
    pallas_call x1, Pallas kernels, local(): pl.pallas_call(functools.partial(kernel, nz=nz), out_shape=jax.ShapeDtype...  66 us
    unnamed x1, local copies, waits for them, and re-layouts  2.26 us

profile of v1, /device:TPU:1, one launch (start us, length us, event | category | flops | bytes accessed | tf_op | source)
XLA Modules:
  0.0 68.9 jit_solution(17289981101201571043)
XLA Ops:
  0.7 66.0 %shard_map.73 = f32[1024,256]{1,0:T(8,128)} custom-call(s32[12]{0:T(128)} %bitcast.5, s32[1]{0:T(128)} %bitcast.3.cnt_ref, bf16[128,8,256]{2,1,0:T(8,128)(2,1)} %inc_hbm.1, bf16[76,8,512]{2,1,0:T(8,128)(2,1)} %past_hbm.1, bf16[8,512,256]{2,1,0:T(8,128)(2,1)} %ker_hbm.1, f32[2,256,256]{2,1,0:T(8,128)} %cpl_hbm.1, f32[256,256]{1,0:T(8,128)} %inv_hbm.1), custom_call_target="tpu_custom_call" | custom-call | tf_op jit(solution)/shard_map/pallas_call | solution.py:459
  66.6 2.3 %copy.10 = f32[128,8,256]{2,1,0:T(8,128)} copy(f32[128,8,256]{2,1,0:T(8,128)} %bitcast.4) | data formatting | bytes 2097152

commit v2 on v1

--- a/solution.py
+++ b/solution.py
@@ -35,7 +35,7 @@
     inc_v, past_v, ker_v, cpl_v, inv_v, hist, part, abuf, ssum, bsend, brecv,
     tab_hi, tab_lo, mat_hi, mat_lo, pads, shifts, drive, state, tsend, pieces, outbuf, obuf,
     load_sem, a_send, a_recv, b_send, b_recv, st_send, st_recv, t_send, p_recv,
-    y_send, x_send, o_send, o_recv, f_send, out_sem,
+    px_recv, early_recv, r_send, y_send, x_send, o_send, o_recv, f_send, f_recv, out_sem,
     *, nz,
 ):
     slots, cols, rows = ker_v.shape
@@ -63,6 +63,15 @@
 
     partner = at(y, x, z, oc)
 
+    past_load = pltpu.make_async_copy(past_hbm, past_v, load_sem.at[0])
+    cpl_load = pltpu.make_async_copy(cpl_hbm, cpl_v, load_sem.at[1])
+    inv_load = pltpu.make_async_copy(inv_hbm, inv_v, load_sem.at[2])
+    inc_load = pltpu.make_async_copy(inc_hbm, inc_v, load_sem.at[3])
+    past_load.start()
+    for q in range(slots):
+        pltpu.make_async_copy(ker_hbm.at[q], ker_v.at[q], load_sem.at[4]).start()
+    ker_load = pltpu.make_async_copy(ker_hbm, ker_v, load_sem.at[4])
+
     barrier = pltpu.get_barrier_semaphore()
 
     def greet(dev):
@@ -84,38 +93,19 @@
         def _():
             greet(at(y, 2 * c + xs, z, c))
 
-    loads_list = [
-        pltpu.make_async_copy(past_hbm, past_v, load_sem.at[0]),
-        pltpu.make_async_copy(cpl_hbm, cpl_v, load_sem.at[1]),
-        pltpu.make_async_copy(inv_hbm, inv_v, load_sem.at[2]),
-        pltpu.make_async_copy(inc_hbm, inc_v, load_sem.at[3]),
-    ]
-    ker_loads = [
-        pltpu.make_async_copy(ker_hbm.at[q], ker_v.at[q], load_sem.at[4 + q]) for q in range(slots)
-    ]
-    loads_list[0].start()
-    for copy in ker_loads:
+        @pl.when((x + 2) % X == 2 * c + xs)
+        def _():
+            greet(at(y, (x + 1) % X, z, c))
+
+    hist[0, :, history * loads:, :] = jnp.zeros((cols // LANE, block * loads, LANE), F32)
+
+    past_load.wait()
+    for copy in (cpl_load, inv_load, inc_load):
         copy.start()
-    for copy in loads_list[1:]:
-        copy.start()
-
-    for blk in range(BLOCKS):
-        hist[blk, :, history * loads:, :] = jnp.zeros((cols // LANE, block * loads, LANE), F32)
-    pads[:, :half, :] = jnp.zeros((2, half, rows), F32)
-
-    @pl.when(c == 0)
-    def _():
-        state[0] = jnp.zeros_like(state[0])
-
-    tab_hi[0:rows, :] = jnp.zeros((rows, rows), BF16)
-    tab_lo[0:rows, :] = jnp.zeros((rows, rows), BF16)
-
-    loads_list[0].wait()
     for part_at in range(cols // LANE):
         lanes = slice(part_at * LANE, (part_at + 1) * LANE)
-        earlier_steps = past_v[:, :, lanes].astype(F32).reshape(history * loads, LANE)
-        hist[0, part_at, 0:history * loads, :] = earlier_steps
-        hist[1, part_at, 0:lead * loads, :] = earlier_steps[block * loads:]
+        hist[0, part_at, 0:history * loads, :] = (
+            past_v[:, :, lanes].astype(F32).reshape(history * loads, LANE))
 
     def put(place, value):
         hi, lo = split(value)
@@ -125,25 +115,27 @@
     def mat(place):
         return mat_hi[place], mat_lo[place]
 
-    loads_list[1].wait()
-    loads_list[2].wait()
+    cpl_load.wait()
+    inv_load.wait()
     put(C1, cpl_v[0])
     put(C2, cpl_v[1])
     put(INV, inv_v[...])
-    for copy in ker_loads:
-        copy.wait()
+    ker_load.wait()
 
     def far(blk, h):
-        total = None
+        windows = []
         for q in range(slots):
             used = lax.max(lax.min(cnt_ref[0] - q, jnp.int32(1)), jnp.int32(0))
             first = history + used * (lead - history - off_ref[q]) + h * half
             place = pl.ds(first * loads, hrows)
-            window = jnp.concatenate(
-                [hist[blk, k, place, :].astype(BF16) for k in range(cols // LANE)], 1)
-            term = dot(window, ker_v[q])
-            total = term if total is None else total + term
-        part[blk, pl.ds(pl.multiple_of(h * hrows, hrows), hrows), :] = total
+            windows += [hist[blk, k, place, :].astype(BF16) for k in range(cols // LANE)]
+        part[blk, pl.ds(pl.multiple_of(h * hrows, hrows), hrows), :] = dot(
+            jnp.concatenate(windows, 1), ker_v[...].reshape(slots * cols, rows))
+
+    def far_whole(h):
+        @pl.when(t >= 0)
+        def _():
+            far(1, h)
 
     held = jnp.logical_and(z == y, member)
 
@@ -156,7 +148,10 @@
     second_term = dot3(last, mat(C2))
 
     def far_first(h):
-        far(0, h)
+        @pl.when(t >= 0)
+        def _():
+            far(0, h)
+
         keep = jnp.where(jnp.logical_and(held, h == 0), 1.0, 0.0).astype(F32)
         base = pl.multiple_of(h * hrows, hrows)
         part[0, pl.ds(base, loads), :] = part[0, pl.ds(base, loads), :] + keep * first_term
@@ -165,13 +160,9 @@
 
     far_first(oc)
 
-    @pl.when(member)
-    def _():
-        pl.semaphore_wait(barrier, nz + 1 + ny - 1 + X - 1)
-
-    @pl.when(jnp.logical_not(member))
-    def _():
-        pl.semaphore_wait(barrier, nz + 1)
+    relayer = jnp.logical_or((x + 1) % X == 2 * c, (x + 1) % X == 2 * c + 1)
+    peers = nz + 1 + jnp.where(member, ny - 1 + X - 1, 0) + jnp.where(relayer, 1, 0)
+    pl.semaphore_wait(barrier, peers)
 
     def pair_copy(blk):
         other = pl.ds(pl.multiple_of(oc * hrows, hrows), hrows)
@@ -182,13 +173,13 @@
 
     def ring_send(blk, dz):
         there = (z + dz) % nz
-        return remote(bsend.at[blk, there], brecv.at[blk, z], b_send.at[blk, dz], b_recv.at[blk, z],
+        return remote(bsend.at[blk, there], brecv.at[blk, z], b_send.at[blk], b_recv.at[blk],
                       at(y, x, there, c))
 
-    def ring_arrival(blk, dz):
-        there = (z + nz - dz) % nz
-        return remote(bsend.at[blk, there], brecv.at[blk, there], b_send.at[blk, dz],
-                      b_recv.at[blk, there], at(y, x, there, c))
+    def ring_all(blk):
+        every = pl.ds(0, nz - 1)
+        return remote(bsend.at[blk, every], brecv.at[blk, every], b_send.at[blk], b_recv.at[blk],
+                      partner)
 
     far_order = sorted(range(1, nz), key=lambda dz: -min(dz, nz - dz))
     near_order = sorted(range(1, nz), key=lambda dz: min(dz, nz - dz))
@@ -207,12 +198,12 @@
 
     def reduce_finish(blk):
         total = bsend[blk, z]
-        for dz in near_order:
-            ring_arrival(blk, dz).wait_recv()
-            total = total + brecv[blk, (z + nz - dz) % nz]
+        ring_all(blk).wait_recv()
+        for dz in range(1, nz):
+            total = total + brecv[blk, (z + dz) % nz]
         return total
 
-    loads_list[3].wait()
+    inc_load.wait()
     row_at = lax.broadcasted_iota(jnp.int32, (half, hrows), 0) * loads + z
     pick = (row_at == lax.broadcasted_iota(jnp.int32, (half, hrows), 1)).astype(BF16)
     for blk in range(BLOCKS):
@@ -220,6 +211,13 @@
         drive[blk] = dot(pick, steps.astype(BF16))
 
     reduce_start(0)
+
+    hist[1, :, history * loads:, :] = jnp.zeros((cols // LANE, block * loads, LANE), F32)
+    hist[1, :, 0:lead * loads, :] = hist[0, :, block * loads:history * loads, :]
+    pads[:, :half, :] = jnp.zeros((2, half, rows), F32)
+
+    tab_hi[0:rows, :] = jnp.zeros((rows, rows), BF16)
+    tab_lo[0:rows, :] = jnp.zeros((rows, rows), BF16)
 
     def table_put(first, count, value):
         hi, lo = split(value)
@@ -275,14 +273,8 @@
         def _():
             copy.wait_send()
 
-    def solve(blk):
-        drive[blk] = drive[blk] - reduce_finish(blk)
-        if blk == 0:
-            state_wait(0)
-        else:
-            state_wait(1)
-            state_wait(2)
-        from_state = split(state[blk])
+    def respond(blk, from_state):
+        from_state = split(from_state)
         by_one, by_two = dot3(from_state, mat(C1)), dot3(from_state, mat(C2))
         row = lax.broadcasted_iota(jnp.int32, by_one.shape, 0)
         change = jnp.where(row == 0, pltpu.roll(by_one, 1, 0), 0.0)
@@ -298,13 +290,23 @@
         both = dot(shifts[...], tab_hi[rows:, :])
         outbuf[blk, c, z] = both[:half] + both[half:] + dot(shifts[0:half, :], tab_lo[rows:, :])
 
-    solve(0)
+    drive[0] = drive[0] - reduce_finish(0)
+
+    @pl.when(c == 0)
+    def _():
+        respond(0, jnp.zeros((8, rows), F32))
+
+    @pl.when(c == 1)
+    def _():
+        state_wait(0)
+        respond(0, state[0])
+
     state_start(0)
     state_start(1)
 
     def turn_copy():
         dst = pieces.at[c, xs_own, z]
-        return remote(tsend, dst, t_send.at[0], p_recv.at[c, xs_own, z],
+        return remote(tsend, dst, t_send.at[0], p_recv.at[c, z],
                       at((2 * y + nz // 2 + nz - z) % ny, x, y, x // 2))
 
     tsend[...] = outbuf[0, c, z].astype(BF16)
@@ -313,37 +315,87 @@
     def load_of(y_):
         return (2 * z + nz // 2 + nz - y_) % nz
 
-    def piece(h, xs, load, ssem, dev):
+    def arrived(h, load):
+        ref = pieces.at[h, xs_own, load]
+        remote(ref, ref, t_send.at[0], p_recv.at[h, load], partner).wait_recv()
+
+    def along_y(h, dy):
+        load = load_of(y)
+        ref = pieces.at[h, xs_own, load]
+        return remote(ref, ref, y_send.at[h], p_recv.at[h, load], at((y + dy) % ny, x, z, c))
+
+    def along_x(h, dy, dx):
+        ref = pieces.at[h, xs_own, load_of((y + ny - dy) % ny)]
+        return remote(ref, ref, x_send.at[h, dx - 1], px_recv.at[h, xs_own],
+                      at(y, (x + dx) % X, z, c))
+
+    def all_x(h, xs, dx):
+        ref = pieces.at[h, xs]
+        return remote(ref, ref, x_send.at[h, dx - 1], px_recv.at[h, xs], partner)
+
+    y_order = [0] + near_order
+    by_left, direct = y_order[:ny // 2], y_order[ny // 2:]
+
+    def early(h, xs, dy, dev):
+        load = load_of((y + ny - dy) % ny)
         ref = pieces.at[h, xs, load]
-        return remote(ref, ref, ssem, p_recv.at[h, xs, load], dev)
-
-    def along_y(h, dy):
-        return piece(h, xs_own, load_of(y), y_send.at[h, dy], at((y + dy) % ny, x, z, c))
-
-    def along_x(h, dy, dx):
+        return remote(ref, ref, r_send.at[h], early_recv.at[h, dy], dev)
+
+    def to_left(h, dy):
         load = load_of((y + ny - dy) % ny)
-        return piece(h, xs_own, load, x_send.at[h, dy, dx], at(y, (x + dx) % X, z, c))
+        ref = pieces.at[h, xs_own, load]
+        return remote(ref, ref, x_send.at[h, X - 2], early_recv.at[h, dy],
+                      at(y, (x + X - 1) % X, z, c))
+
+    def relays(h):
+        for xs in range(2):
+            @pl.when((x + 1) % X == 2 * c + xs)
+            def _():
+                for dy in by_left:
+                    early(h, xs, dy, partner).wait_recv()
+                    early_on(h, xs, dy).start()
+
+    def early_on(h, xs, dy):
+        load = load_of((y + ny - dy) % ny)
+        ref = pieces.at[h, xs, load]
+        return remote(ref, ref, r_send.at[h], px_recv.at[h, xs], at(y, (x + X - 1) % X, z, c))
+
+    def handed_on(h):
+        some = pieces.at[h, 0, pl.ds(0, ny - 1)]
+        remote(some, some, y_send.at[h], p_recv.at[h, 0], partner).wait_send()
+        all_x(h, 0, 1).wait_send()
+        all_x(h, 0, 3).wait_send()
+        later = pieces.at[h, 0, pl.ds(0, len(direct))]
+        remote(later, later, x_send.at[h, 1], p_recv.at[h, 0], partner).wait_send()
 
     def hand_on(h):
         @pl.when(member)
         def _():
-            piece(h, xs_own, load_of(y), y_send.at[h, 0], partner).wait_recv()
+            arrived(h, load_of(y))
             for dy in far_order:
                 along_y(h, dy).start()
-            for dx in (2, 1, 3):
-                along_x(h, 0, dx).start()
-            for dy in near_order:
-                load = load_of((y + ny - dy) % ny)
-                piece(h, xs_own, load, y_send.at[h, dy], partner).wait_recv()
-                for dx in (2, 1, 3):
-                    along_x(h, dy, dx).start()
+            for dy in y_order:
+                if dy > 0:
+                    arrived(h, load_of((y + ny - dy) % ny))
+                if dy in by_left:
+                    to_left(h, dy).start()
+                    along_x(h, dy, 1).start()
+                else:
+                    for dx in (2, 1, 3):
+                        along_x(h, dy, dx).start()
 
     def take_in(h):
         for xs in range(2):
-            @pl.when(2 * c + xs != x)
+            delta = (x + X - 2 * c - xs) % X
+
+            @pl.when(jnp.logical_or(delta == 1, delta == 2))
             def _():
-                for load in range(loads):
-                    piece(h, xs, load, x_send.at[h, 0, 0], partner).wait_recv()
+                all_x(h, xs, 1).wait_recv()
+
+            @pl.when(delta == 3)
+            def _():
+                later = pieces.at[h, xs, pl.ds(0, len(direct))]
+                remote(later, later, r_send.at[h], px_recv.at[h, xs], partner).wait_recv()
         for xs in range(2):
             for load in range(loads):
                 to = pl.ds((lead + h * half) * loads + load, half, stride=loads)
@@ -351,48 +403,68 @@
                     part_of = pieces[h, xs, load, :, k * LANE:(k + 1) * LANE]
                     hist[1, xs * (rows // LANE) + k, to, :] = part_of.astype(F32)
 
+    def direct_sem(blk, from_z):
+        return o_recv.at[0] if blk == 0 else o_recv.at[1 + from_z]
+
     def own_copy(blk, dz):
         ref = outbuf.at[blk, c, z]
         there = (z + dz) % nz
-        return remote(ref, ref, o_send.at[blk, dz], o_recv.at[blk, c, z], at(y, x, there, c))
-
-    def cross_copy(blk, h, from_z, dz):
-        ref = outbuf.at[blk, h, from_z]
-        return remote(ref, ref, f_send.at[blk, dz], o_recv.at[blk, h, from_z], partner)
+        return remote(ref, ref, o_send.at[blk], direct_sem(blk, z), at(y, x, there, c))
+
+    def own_all(blk):
+        some = outbuf.at[blk, c, pl.ds(0, nz - 1)]
+        return remote(some, some, o_send.at[blk], o_recv.at[0], partner)
+
+    def own_arrival(blk, from_z):
+        ref = outbuf.at[blk, c, from_z]
+        remote(ref, ref, o_send.at[blk], direct_sem(blk, from_z), partner).wait_recv()
+
+    def cross_copy(blk, from_z):
+        ref = outbuf.at[blk, c, from_z]
+        return remote(ref, ref, f_send.at[blk], f_recv.at[blk], partner)
+
+    def cross_all(blk, h):
+        ref = outbuf.at[blk, h]
+        return remote(ref, ref, f_send.at[blk], f_recv.at[blk], partner)
 
     def spread_start(blk):
         for dz in far_order:
             own_copy(blk, dz).start()
-        cross_copy(blk, c, z, 0).start()
+        cross_copy(blk, z).start()
 
     def spread_cross(blk):
+        if blk == 0:
+            own_all(blk).wait_recv()
         for dz in near_order:
             from_z = (z + nz - dz) % nz
-            cross_copy(blk, c, from_z, dz).wait_recv()
-            cross_copy(blk, c, from_z, dz).start()
-
-    def spread_finish(blk):
-        for dz in range(nz):
-            cross_copy(blk, oc, (z + nz - dz) % nz, dz).wait_recv()
-
-    def out_copy(blk, k):
-        place = pl.ds(blk * block * loads, block * loads)
+            if blk == 1:
+                own_arrival(blk, from_z)
+            cross_copy(blk, from_z).start()
+
+    def spread_sent(blk):
+        own_all(blk).wait_send()
+        cross_all(blk, 0).wait_send()
+
+    def out_copy(blk, h, k):
+        first = pl.multiple_of((blk * block + h * half) * loads, loads)
+        place = pl.ds(first, hrows)
         return pltpu.make_async_copy(
-            obuf.at[k, place], out_hbm.at[place, pl.ds(k * LANE, LANE)], out_sem.at[blk, k])
-
-    def interleave(blk):
+            obuf.at[k, place], out_hbm.at[place, pl.ds(k * LANE, LANE)], out_sem.at[blk, h, k])
+
+    def out_start(blk, h):
         for k in range(rows // LANE):
-            for h in range(2):
-                for load in range(loads):
-                    to = pl.ds((blk * block + h * half) * loads + load, half, stride=loads)
-                    obuf[k, to, :] = outbuf[blk, h, load, :, k * LANE:(k + 1) * LANE]
-            out_copy(blk, k).start()
+            for load in range(loads):
+                to = pl.ds((blk * block + h * half) * loads + load, half, stride=loads)
+                obuf[k, to, :] = outbuf[blk, h, load, :, k * LANE:(k + 1) * LANE]
+            out_copy(blk, h, k).start()
 
     hand_on(0)
+    relays(0)
     hand_on(1)
+    relays(1)
     spread_start(0)
     take_in(0)
-    far(1, 0)
+    far_whole(0)
 
     @pl.when(c == 1)
     def _():
@@ -403,7 +475,7 @@
         reduce_start(1)
 
     take_in(1)
-    far(1, 1)
+    far_whole(1)
 
     @pl.when(c == 0)
     def _():
@@ -414,37 +486,61 @@
         reduce_start(1)
 
     spread_cross(0)
-    spread_finish(0)
-    interleave(0)
-
-    solve(1)
-    state_start(2)
-    spread_start(1)
-    spread_cross(1)
-    spread_finish(1)
-    interleave(1)
-
+    ring_all(0).wait_send()
     for blk in range(BLOCKS):
         pair_copy(blk).wait_send()
-        for dz in range(1, nz):
-            ring_send(blk, dz).wait_send()
-            own_copy(blk, dz).wait_send()
-        for dz in range(nz):
-            cross_copy(blk, c, (z + nz - dz) % nz, dz).wait_send()
-        for k in range(rows // LANE):
-            out_copy(blk, k).wait()
-    for which in range(3):
+    turn_copy().wait_send()
+    for which in range(2):
         state_sent(which)
-    turn_copy().wait_send()
 
     @pl.when(member)
     def _():
         for h in range(2):
-            for dy in range(1, ny):
-                along_y(h, dy).wait_send()
-            for dy in range(ny):
-                for dx in range(1, X):
-                    along_x(h, dy, dx).wait_send()
+            handed_on(h)
+
+    @pl.when(relayer)
+    def _():
+        for h in range(2):
+            some = pieces.at[h, 0, pl.ds(0, len(by_left))]
+            remote(some, some, r_send.at[h], px_recv.at[h, 0], partner).wait_send()
+
+    drive[1] = drive[1] - reduce_finish(1)
+    state_wait(1)
+    state_wait(2)
+
+    @pl.when(t >= 0)
+    def _():
+        respond(1, state[1])
+
+    spread_start(1)
+    state_start(2)
+
+    cross_all(0, oc).wait_recv()
+    spread_sent(0)
+    ring_all(1).wait_send()
+    for h in range(2):
+        out_start(0, h)
+    state_sent(2)
+
+    spread_cross(1)
+
+    @pl.when(c == 1)
+    def _():
+        cross_all(1, 0).wait_recv()
+        out_start(1, 0)
+        out_start(1, 1)
+
+    @pl.when(c == 0)
+    def _():
+        out_start(1, 0)
+        cross_all(1, 1).wait_recv()
+        out_start(1, 1)
+
+    spread_sent(1)
+    for k in range(rows // LANE):
+        for blk in range(BLOCKS):
+            for h in range(2):
+                out_copy(blk, h, k).wait()
 
 
 def local(nz, incident, past_density, kernels, lag_offset, lag_counts, couplings, inverse):
@@ -486,21 +582,25 @@
             vmem((2, 2, loads, half, rows), BF16),
             vmem((BLOCKS, 2, nz, half, rows), F32),
             vmem((rows // LANE, steps * loads, LANE), F32),
-            dma((4 + slots,)),
+            dma((5,)),
             dma((BLOCKS,)),
             dma((BLOCKS,)),
-            dma((BLOCKS, nz)),
-            dma((BLOCKS, nz)),
+            dma((BLOCKS,)),
+            dma((BLOCKS,)),
             dma((3,)),
             dma((3,)),
             dma((1,)),
-            dma((2, 2, loads)),
+            dma((2, loads)),
+            dma((2, 2)),
             dma((2, nz)),
-            dma((2, nz, X)),
-            dma((BLOCKS, nz)),
-            dma((BLOCKS, 2, nz)),
-            dma((BLOCKS, nz)),
-            dma((BLOCKS, rows // LANE)),
+            dma((2,)),
+            dma((2,)),
+            dma((2, X - 1)),
+            dma((BLOCKS,)),
+            dma((1 + nz,)),
+            dma((BLOCKS,)),
+            dma((BLOCKS,)),
+            dma((BLOCKS, 2, rows // LANE)),
         ],
         compiler_params=pltpu.CompilerParams(
             collective_id=0, has_side_effects=True, vmem_limit_bytes=60 * 1024 * 1024),

time: 69.1 us -> 72.7 us (1.052); the launches traced: 68.9 us -> 71.4 us
  Pallas kernels: 66 us -> 68.4 us
    pallas_call x1, Pallas kernels: 66 us -> 68.4 us  [local(): pl.pallas_call(functools.partial(kernel, nz=nz), out_shape=jax.ShapeDtype...]
where the time goes in v2:
time: 72.7 us; the launch traced here: 71.4 us
  Pallas kernels  68.4 us (94%)
  local copies, waits for them, and re-layouts  2.26 us (3%)
    pallas_call x1, Pallas kernels, local(): pl.pallas_call(functools.partial(kernel, nz=nz), out_shape=jax.ShapeDtype...  68.4 us
    unnamed x1, local copies, waits for them, and re-layouts  2.26 us

profile of v2, /device:TPU:1, one launch (start us, length us, event | category | flops | bytes accessed | tf_op | source)
XLA Modules:
  0.0 71.4 jit_solution(12885842351354401080)
XLA Ops:
  0.7 68.4 %shard_map.73 = f32[1024,256]{1,0:T(8,128)} custom-call(s32[12]{0:T(128)} %bitcast.5, s32[1]{0:T(128)} %bitcast.3.cnt_ref, bf16[128,8,256]{2,1,0:T(8,128)(2,1)} %inc_hbm.1, bf16[76,8,512]{2,1,0:T(8,128)(2,1)} %past_hbm.1, bf16[8,512,256]{2,1,0:T(8,128)(2,1)} %ker_hbm.1, f32[2,256,256]{2,1,0:T(8,128)} %cpl_hbm.1, f32[256,256]{1,0:T(8,128)} %inv_hbm.1), custom_call_target="tpu_custom_call" | custom-call | tf_op jit(solution)/shard_map/pallas_call | solution.py:555
  69.1 2.3 %copy.10 = f32[128,8,256]{2,1,0:T(8,128)} copy(f32[128,8,256]{2,1,0:T(8,128)} %bitcast.4) | data formatting | bytes 2097152

commit v3 on v2

--- a/solution.py
+++ b/solution.py
@@ -35,7 +35,7 @@
     inc_v, past_v, ker_v, cpl_v, inv_v, hist, part, abuf, ssum, bsend, brecv,
     tab_hi, tab_lo, mat_hi, mat_lo, pads, shifts, drive, state, tsend, pieces, outbuf, obuf,
     load_sem, a_send, a_recv, b_send, b_recv, st_send, st_recv, t_send, p_recv,
-    px_recv, early_recv, r_send, y_send, x_send, o_send, o_recv, f_send, f_recv, out_sem,
+    px_recv, y_send, x_send, o_send, o_recv, f_send, f_recv, out_sem,
     *, nz,
 ):
     slots, cols, rows = ker_v.shape
@@ -71,6 +71,8 @@
     for q in range(slots):
         pltpu.make_async_copy(ker_hbm.at[q], ker_v.at[q], load_sem.at[4]).start()
     ker_load = pltpu.make_async_copy(ker_hbm, ker_v, load_sem.at[4])
+    for copy in (cpl_load, inv_load, inc_load):
+        copy.start()
 
     barrier = pltpu.get_barrier_semaphore()
 
@@ -93,19 +95,15 @@
         def _():
             greet(at(y, 2 * c + xs, z, c))
 
-        @pl.when((x + 2) % X == 2 * c + xs)
-        def _():
-            greet(at(y, (x + 1) % X, z, c))
-
     hist[0, :, history * loads:, :] = jnp.zeros((cols // LANE, block * loads, LANE), F32)
 
     past_load.wait()
-    for copy in (cpl_load, inv_load, inc_load):
-        copy.start()
-    for part_at in range(cols // LANE):
-        lanes = slice(part_at * LANE, (part_at + 1) * LANE)
-        hist[0, part_at, 0:history * loads, :] = (
-            past_v[:, :, lanes].astype(F32).reshape(history * loads, LANE))
+    @pl.when(t >= 0)
+    def _():
+        for part_at in range(cols // LANE):
+            lanes = slice(part_at * LANE, (part_at + 1) * LANE)
+            hist[0, part_at, 0:history * loads, :] = (
+                past_v[:, :, lanes].astype(F32).reshape(history * loads, LANE))
 
     def put(place, value):
         hi, lo = split(value)
@@ -160,9 +158,13 @@
 
     far_first(oc)
 
-    relayer = jnp.logical_or((x + 1) % X == 2 * c, (x + 1) % X == 2 * c + 1)
-    peers = nz + 1 + jnp.where(member, ny - 1 + X - 1, 0) + jnp.where(relayer, 1, 0)
-    pl.semaphore_wait(barrier, peers)
+    @pl.when(member)
+    def _():
+        pl.semaphore_wait(barrier, nz + 1 + ny - 1 + X - 1)
+
+    @pl.when(jnp.logical_not(member))
+    def _():
+        pl.semaphore_wait(barrier, nz + 1)
 
     def pair_copy(blk):
         other = pl.ds(pl.multiple_of(oc * hrows, hrows), hrows)
@@ -225,16 +227,18 @@
         tab_hi[place, :] = hi
         tab_lo[place, :] = lo
 
-    put(A1, -dot3(mat(C1), mat(INV)))
-    put(A2, -dot3(mat(C2), mat(INV)))
-    put(Q1, dot3(mat(A1), mat(A1)) + (mat_hi[A2].astype(F32) + mat_lo[A2].astype(F32)))
-    put(Q2, dot3(mat(Q1), mat(A1)) + dot3(mat(A1), mat(A2)))
-    put(Q3, dot3(mat(Q2), mat(A1)) + dot3(mat(Q1), mat(A2)))
-    put(D2, dot3(mat(A2), mat(Q2)))
-    table_put(0, 1, inv_v[...])
-    table_put(1, 1, dot3(mat(INV), mat(A1)))
-    table_put(2, 1, dot3(mat(INV), mat(Q1)))
-    table_put(3, 1, dot3(mat(INV), mat(Q2)))
+    @pl.when(t >= 0)
+    def _():
+        put(A1, -dot3(mat(C1), mat(INV)))
+        put(A2, -dot3(mat(C2), mat(INV)))
+        put(Q1, dot3(mat(A1), mat(A1)) + (mat_hi[A2].astype(F32) + mat_lo[A2].astype(F32)))
+        put(Q2, dot3(mat(Q1), mat(A1)) + dot3(mat(A1), mat(A2)))
+        put(Q3, dot3(mat(Q2), mat(A1)) + dot3(mat(Q1), mat(A2)))
+        put(D2, dot3(mat(A2), mat(Q2)))
+        table_put(0, 1, inv_v[...])
+        table_put(1, 1, dot3(mat(INV), mat(A1)))
+        table_put(2, 1, dot3(mat(INV), mat(Q1)))
+        table_put(3, 1, dot3(mat(INV), mat(Q2)))
 
     def four_more(step, carry):
         one = pl.ds(pl.multiple_of((4 * step - 3) * rows, rows), 4 * rows)
@@ -244,7 +248,9 @@
         table_put(4 * step, 4, value)
         return carry
 
-    lax.fori_loop(1, half // 4, four_more, 0)
+    @pl.when(t >= 0)
+    def _():
+        lax.fori_loop(1, half // 4, four_more, 0)
 
     def state_copy(which):
         blk = which // 2
@@ -333,40 +339,11 @@
         ref = pieces.at[h, xs]
         return remote(ref, ref, x_send.at[h, dx - 1], px_recv.at[h, xs], partner)
 
-    y_order = [0] + near_order
-    by_left, direct = y_order[:ny // 2], y_order[ny // 2:]
-
-    def early(h, xs, dy, dev):
-        load = load_of((y + ny - dy) % ny)
-        ref = pieces.at[h, xs, load]
-        return remote(ref, ref, r_send.at[h], early_recv.at[h, dy], dev)
-
-    def to_left(h, dy):
-        load = load_of((y + ny - dy) % ny)
-        ref = pieces.at[h, xs_own, load]
-        return remote(ref, ref, x_send.at[h, X - 2], early_recv.at[h, dy],
-                      at(y, (x + X - 1) % X, z, c))
-
-    def relays(h):
-        for xs in range(2):
-            @pl.when((x + 1) % X == 2 * c + xs)
-            def _():
-                for dy in by_left:
-                    early(h, xs, dy, partner).wait_recv()
-                    early_on(h, xs, dy).start()
-
-    def early_on(h, xs, dy):
-        load = load_of((y + ny - dy) % ny)
-        ref = pieces.at[h, xs, load]
-        return remote(ref, ref, r_send.at[h], px_recv.at[h, xs], at(y, (x + X - 1) % X, z, c))
-
     def handed_on(h):
         some = pieces.at[h, 0, pl.ds(0, ny - 1)]
         remote(some, some, y_send.at[h], p_recv.at[h, 0], partner).wait_send()
-        all_x(h, 0, 1).wait_send()
-        all_x(h, 0, 3).wait_send()
-        later = pieces.at[h, 0, pl.ds(0, len(direct))]
-        remote(later, later, x_send.at[h, 1], p_recv.at[h, 0], partner).wait_send()
+        for dx in range(1, X):
+            all_x(h, 0, dx).wait_send()
 
     def hand_on(h):
         @pl.when(member)
@@ -374,28 +351,18 @@
             arrived(h, load_of(y))
             for dy in far_order:
                 along_y(h, dy).start()
-            for dy in y_order:
-                if dy > 0:
-                    arrived(h, load_of((y + ny - dy) % ny))
-                if dy in by_left:
-                    to_left(h, dy).start()
-                    along_x(h, dy, 1).start()
-                else:
-                    for dx in (2, 1, 3):
-                        along_x(h, dy, dx).start()
+            for dx in (2, 1, 3):
+                along_x(h, 0, dx).start()
+            for dy in near_order:
+                arrived(h, load_of((y + ny - dy) % ny))
+                for dx in (2, 1, 3):
+                    along_x(h, dy, dx).start()
 
     def take_in(h):
         for xs in range(2):
-            delta = (x + X - 2 * c - xs) % X
-
-            @pl.when(jnp.logical_or(delta == 1, delta == 2))
+            @pl.when(2 * c + xs != x)
             def _():
                 all_x(h, xs, 1).wait_recv()
-
-            @pl.when(delta == 3)
-            def _():
-                later = pieces.at[h, xs, pl.ds(0, len(direct))]
-                remote(later, later, r_send.at[h], px_recv.at[h, xs], partner).wait_recv()
         for xs in range(2):
             for load in range(loads):
                 to = pl.ds((lead + h * half) * loads + load, half, stride=loads)
@@ -459,9 +426,7 @@
             out_copy(blk, h, k).start()
 
     hand_on(0)
-    relays(0)
     hand_on(1)
-    relays(1)
     spread_start(0)
     take_in(0)
     far_whole(0)
@@ -497,12 +462,6 @@
     def _():
         for h in range(2):
             handed_on(h)
-
-    @pl.when(relayer)
-    def _():
-        for h in range(2):
-            some = pieces.at[h, 0, pl.ds(0, len(by_left))]
-            remote(some, some, r_send.at[h], px_recv.at[h, 0], partner).wait_send()
 
     drive[1] = drive[1] - reduce_finish(1)
     state_wait(1)
@@ -592,8 +551,6 @@
             dma((1,)),
             dma((2, loads)),
             dma((2, 2)),
-            dma((2, nz)),
-            dma((2,)),
             dma((2,)),
             dma((2, X - 1)),
             dma((BLOCKS,)),

time: 72.7 us -> 66.6 us (0.916)
  Pallas kernels: 68.4 us -> 62.7 us
    pallas_call x1, Pallas kernels: 68.4 us -> 62.7 us  [local(): pl.pallas_call(functools.partial(kernel, nz=nz), out_shape=jax.ShapeDtype...]
where the time goes in v3:
time: 66.6 us; the launch traced here: 65.6 us
  Pallas kernels  62.7 us (94%)
  local copies, waits for them, and re-layouts  2.26 us (3%)
    pallas_call x1, Pallas kernels, local(): pl.pallas_call(functools.partial(kernel, nz=nz), out_shape=jax.ShapeDtype...  62.7 us
    unnamed x1, local copies, waits for them, and re-layouts  2.26 us

profile of v3, /device:TPU:1, one launch (start us, length us, event | category | flops | bytes accessed | tf_op | source)
XLA Modules:
  0.0 65.6 jit_solution(9620637612461900435)
XLA Ops:
  0.7 62.7 %shard_map.73 = f32[1024,256]{1,0:T(8,128)} custom-call(s32[12]{0:T(128)} %bitcast.5, s32[1]{0:T(128)} %bitcast.3.cnt_ref, bf16[128,8,256]{2,1,0:T(8,128)(2,1)} %inc_hbm.1, bf16[76,8,512]{2,1,0:T(8,128)(2,1)} %past_hbm.1, bf16[8,512,256]{2,1,0:T(8,128)(2,1)} %ker_hbm.1, f32[2,256,256]{2,1,0:T(8,128)} %cpl_hbm.1, f32[256,256]{1,0:T(8,128)} %inv_hbm.1), custom_call_target="tpu_custom_call" | custom-call | tf_op jit(solution)/shard_map/pallas_call | solution.py:514
  63.3 2.3 %copy.10 = f32[128,8,256]{2,1,0:T(8,128)} copy(f32[128,8,256]{2,1,0:T(8,128)} %bitcast.4) | data formatting | bytes 2097152

commit v4 on v3

--- a/solution.py
+++ b/solution.py
@@ -50,7 +50,9 @@
     y, x = t // X, t % X
     z, c = s // 2, s % 2
     oc = 1 - c
-    member = c == x // 2
+    deltas = [(x + X - 2 * c - xs) % X for xs in range(2)]
+    member = [delta < 2 for delta in deltas]
+    left, right = (x + X - 1) % X, (x + 1) % X
     xs_own = x % 2
 
     def at(y_, x_, z_, c_):
@@ -83,17 +85,21 @@
         greet(at(y, x, (z + dz) % nz, c))
     greet(partner)
 
-    @pl.when(member)
-    def _():
-        for core in range(2):
-            greet(at(z, x, (2 * z + nz // 2 + nz - y) % nz, core))
-        for dy in range(1, ny):
-            greet(at((y + dy) % ny, x, z, c))
-
     for xs in range(2):
-        @pl.when(2 * c + xs != x)
-        def _():
-            greet(at(y, 2 * c + xs, z, c))
+        @pl.when(member[xs])
+        def _():
+            for core in range(2):
+                greet(at(z, 2 * c + xs, (2 * z + nz // 2 + nz - y) % nz, core))
+            for dy in range(1, ny):
+                greet(at((y + dy) % ny, x, z, c))
+
+        @pl.when(deltas[xs] == 2)
+        def _():
+            greet(at(y, left, z, c))
+
+        @pl.when(deltas[xs] == 3)
+        def _():
+            greet(at(y, right, z, c))
 
     hist[0, :, history * loads:, :] = jnp.zeros((cols // LANE, block * loads, LANE), F32)
 
@@ -135,7 +141,7 @@
         def _():
             far(1, h)
 
-    held = jnp.logical_and(z == y, member)
+    held = jnp.logical_and(z == y, c == x // 2)
 
     def earlier(step):
         both = past_v[step].astype(F32)
@@ -158,13 +164,10 @@
 
     far_first(oc)
 
-    @pl.when(member)
-    def _():
-        pl.semaphore_wait(barrier, nz + 1 + ny - 1 + X - 1)
-
-    @pl.when(jnp.logical_not(member))
-    def _():
-        pl.semaphore_wait(barrier, nz + 1)
+    peers = nz + 2
+    for xs in range(2):
+        peers = peers + jnp.where(member[xs], ny, 0)
+    pl.semaphore_wait(barrier, peers)
 
     def pair_copy(blk):
         other = pl.ds(pl.multiple_of(oc * hrows, hrows), hrows)
@@ -310,59 +313,64 @@
     state_start(0)
     state_start(1)
 
-    def turn_copy():
-        dst = pieces.at[c, xs_own, z]
-        return remote(tsend, dst, t_send.at[0], p_recv.at[c, z],
-                      at((2 * y + nz // 2 + nz - z) % ny, x, y, x // 2))
+    def turn_copy(column):
+        return remote(tsend, pieces.at[c, xs_own, z], t_send.at[column], p_recv.at[c, xs_own, z],
+                      at((2 * y + nz // 2 + nz - z) % ny, (x + column) % X, y, x // 2))
 
     tsend[...] = outbuf[0, c, z].astype(BF16)
-    turn_copy().start()
+    for column in (1, 0):
+        turn_copy(column).start()
 
     def load_of(y_):
         return (2 * z + nz // 2 + nz - y_) % nz
 
-    def arrived(h, load):
-        ref = pieces.at[h, xs_own, load]
-        remote(ref, ref, t_send.at[0], p_recv.at[h, load], partner).wait_recv()
-
-    def along_y(h, dy):
+    def arrived(h, xs, load):
+        ref = pieces.at[h, xs, load]
+        remote(ref, ref, t_send.at[0], p_recv.at[h, xs, load], partner).wait_recv()
+
+    def along_y(h, xs, dy):
         load = load_of(y)
-        ref = pieces.at[h, xs_own, load]
-        return remote(ref, ref, y_send.at[h], p_recv.at[h, load], at((y + dy) % ny, x, z, c))
-
-    def along_x(h, dy, dx):
-        ref = pieces.at[h, xs_own, load_of((y + ny - dy) % ny)]
-        return remote(ref, ref, x_send.at[h, dx - 1], px_recv.at[h, xs_own],
-                      at(y, (x + dx) % X, z, c))
-
-    def all_x(h, xs, dx):
+        ref = pieces.at[h, xs, load]
+        return remote(ref, ref, y_send.at[h, xs], p_recv.at[h, xs, load],
+                      at((y + dy) % ny, x, z, c))
+
+    def along_x(h, xs, dy):
+        ref = pieces.at[h, xs, load_of((y + ny - dy) % ny)]
+        to = jnp.where(deltas[xs] == 0, left, right)
+        return remote(ref, ref, x_send.at[h, xs], px_recv.at[h, xs], at(y, to, z, c))
+
+    def all_x(h, xs):
         ref = pieces.at[h, xs]
-        return remote(ref, ref, x_send.at[h, dx - 1], px_recv.at[h, xs], partner)
+        return remote(ref, ref, x_send.at[h, xs], px_recv.at[h, xs], partner)
 
     def handed_on(h):
-        some = pieces.at[h, 0, pl.ds(0, ny - 1)]
-        remote(some, some, y_send.at[h], p_recv.at[h, 0], partner).wait_send()
-        for dx in range(1, X):
-            all_x(h, 0, dx).wait_send()
+        for xs in range(2):
+            @pl.when(member[xs])
+            def _():
+                some = pieces.at[h, xs, pl.ds(0, ny - 1)]
+                remote(some, some, y_send.at[h, xs], p_recv.at[h, xs, 0], partner).wait_send()
+                all_x(h, xs).wait_send()
 
     def hand_on(h):
-        @pl.when(member)
-        def _():
-            arrived(h, load_of(y))
-            for dy in far_order:
-                along_y(h, dy).start()
-            for dx in (2, 1, 3):
-                along_x(h, 0, dx).start()
-            for dy in near_order:
-                arrived(h, load_of((y + ny - dy) % ny))
-                for dx in (2, 1, 3):
-                    along_x(h, dy, dx).start()
+        for xs in range(2):
+            @pl.when(member[xs])
+            def _():
+                arrived(h, xs, load_of(y))
+                for dy in far_order:
+                    along_y(h, xs, dy).start()
+                along_x(h, xs, 0).start()
+        for dy in near_order:
+            for xs in range(2):
+                @pl.when(member[xs])
+                def _():
+                    arrived(h, xs, load_of((y + ny - dy) % ny))
+                    along_x(h, xs, dy).start()
 
     def take_in(h):
         for xs in range(2):
-            @pl.when(2 * c + xs != x)
+            @pl.when(jnp.logical_not(member[xs]))
             def _():
-                all_x(h, xs, 1).wait_recv()
+                all_x(h, xs).wait_recv()
         for xs in range(2):
             for load in range(loads):
                 to = pl.ds((lead + h * half) * loads + load, half, stride=loads)
@@ -454,14 +462,13 @@
     ring_all(0).wait_send()
     for blk in range(BLOCKS):
         pair_copy(blk).wait_send()
-    turn_copy().wait_send()
+    for column in range(2):
+        turn_copy(column).wait_send()
     for which in range(2):
         state_sent(which)
 
-    @pl.when(member)
-    def _():
-        for h in range(2):
-            handed_on(h)
+    for h in range(2):
+        handed_on(h)
 
     drive[1] = drive[1] - reduce_finish(1)
     state_wait(1)
@@ -548,11 +555,11 @@
             dma((BLOCKS,)),
             dma((3,)),
             dma((3,)),
-            dma((1,)),
-            dma((2, loads)),
+            dma((2,)),
+            dma((2, 2, loads)),
             dma((2, 2)),
-            dma((2,)),
-            dma((2, X - 1)),
+            dma((2, 2)),
+            dma((2, 2)),
             dma((BLOCKS,)),
             dma((1 + nz,)),
             dma((BLOCKS,)),

time: 66.6 us -> 71.4 us (1.072)
  Pallas kernels: 62.7 us -> 67.5 us
    pallas_call x1, Pallas kernels: 62.7 us -> 67.5 us  [local(): pl.pallas_call(functools.partial(kernel, nz=nz), out_shape=jax.ShapeDtype...]
where the time goes in v4:
time: 71.4 us; the launch traced here: 70.4 us
  Pallas kernels  67.5 us (95%)
  local copies, waits for them, and re-layouts  2.26 us (3%)
    pallas_call x1, Pallas kernels, local(): pl.pallas_call(functools.partial(kernel, nz=nz), out_shape=jax.ShapeDtype...  67.5 us
    unnamed x1, local copies, waits for them, and re-layouts  2.26 us

profile of v4, /device:TPU:1, one launch (start us, length us, event | category | flops | bytes accessed | tf_op | source)
XLA Modules:
  0.0 70.4 jit_solution(7850744744989556526)
XLA Ops:
  0.7 67.5 %shard_map.73 = f32[1024,256]{1,0:T(8,128)} custom-call(s32[12]{0:T(128)} %bitcast.5, s32[1]{0:T(128)} %bitcast.3.cnt_ref, bf16[128,8,256]{2,1,0:T(8,128)(2,1)} %inc_hbm.1, bf16[76,8,512]{2,1,0:T(8,128)(2,1)} %past_hbm.1, bf16[8,512,256]{2,1,0:T(8,128)(2,1)} %ker_hbm.1, f32[2,256,256]{2,1,0:T(8,128)} %cpl_hbm.1, f32[256,256]{1,0:T(8,128)} %inv_hbm.1), custom_call_target="tpu_custom_call" | custom-call | tf_op jit(solution)/shard_map/pallas_call | solution.py:521
  68.1 2.3 %copy.10 = f32[128,8,256]{2,1,0:T(8,128)} copy(f32[128,8,256]{2,1,0:T(8,128)} %bitcast.4) | data formatting | bytes 2097152

commit v5 on v3

--- a/solution.py
+++ b/solution.py
@@ -33,7 +33,7 @@
 def kernel(
     off_ref, cnt_ref, inc_hbm, past_hbm, ker_hbm, cpl_hbm, inv_hbm, out_hbm,
     inc_v, past_v, ker_v, cpl_v, inv_v, hist, part, abuf, ssum, bsend, brecv,
-    tab_hi, tab_lo, mat_hi, mat_lo, pads, shifts, drive, state, tsend, pieces, outbuf, obuf,
+    terms, tab_hi, tab_lo, mat_hi, mat_lo, pads, shifts, drive, state, tsend, pieces, outbuf, obuf,
     load_sem, a_send, a_recv, b_send, b_recv, st_send, st_recv, t_send, p_recv,
     px_recv, y_send, x_send, o_send, o_recv, f_send, f_recv, out_sem,
     *, nz,
@@ -113,11 +113,6 @@
     def mat(place):
         return mat_hi[place], mat_lo[place]
 
-    cpl_load.wait()
-    inv_load.wait()
-    put(C1, cpl_v[0])
-    put(C2, cpl_v[1])
-    put(INV, inv_v[...])
     ker_load.wait()
 
     def far(blk, h):
@@ -141,22 +136,30 @@
         both = past_v[step].astype(F32)
         return jnp.where(xs_own == 0, both[:, :rows], both[:, rows:])
 
-    last, before = split(earlier(history - 1)), split(earlier(history - 2))
-    first_term = dot3(last, mat(C1)) + dot3(before, mat(C2))
-    second_term = dot3(last, mat(C2))
-
     def far_first(h):
         @pl.when(t >= 0)
         def _():
             far(0, h)
 
+    def state_first(h):
         keep = jnp.where(jnp.logical_and(held, h == 0), 1.0, 0.0).astype(F32)
         base = pl.multiple_of(h * hrows, hrows)
-        part[0, pl.ds(base, loads), :] = part[0, pl.ds(base, loads), :] + keep * first_term
+        part[0, pl.ds(base, loads), :] = part[0, pl.ds(base, loads), :] + keep * terms[0:loads]
         base2 = pl.multiple_of(h * hrows + loads, loads)
-        part[0, pl.ds(base2, loads), :] = part[0, pl.ds(base2, loads), :] + keep * second_term
+        part[0, pl.ds(base2, loads), :] = part[0, pl.ds(base2, loads), :] + keep * terms[loads:]
 
     far_first(oc)
+    cpl_load.wait()
+
+    @pl.when(t >= 0)
+    def _():
+        put(C1, cpl_v[0])
+        put(C2, cpl_v[1])
+        last, before = split(earlier(history - 1)), split(earlier(history - 2))
+        terms[0:loads] = dot3(last, mat(C1)) + dot3(before, mat(C2))
+        terms[loads:] = dot3(last, mat(C2))
+
+    state_first(oc)
 
     @pl.when(member)
     def _():
@@ -172,6 +175,7 @@
 
     pair_copy(0).start()
     far_first(c)
+    state_first(c)
 
     def ring_send(blk, dz):
         there = (z + dz) % nz
@@ -205,6 +209,8 @@
             total = total + brecv[blk, (z + dz) % nz]
         return total
 
+    reduce_start(0)
+
     inc_load.wait()
     row_at = lax.broadcasted_iota(jnp.int32, (half, hrows), 0) * loads + z
     pick = (row_at == lax.broadcasted_iota(jnp.int32, (half, hrows), 1)).astype(BF16)
@@ -212,12 +218,13 @@
         steps = inc_v[pl.ds(blk * block + c * half, half)].astype(F32).reshape(hrows, rows)
         drive[blk] = dot(pick, steps.astype(BF16))
 
-    reduce_start(0)
 
     hist[1, :, history * loads:, :] = jnp.zeros((cols // LANE, block * loads, LANE), F32)
     hist[1, :, 0:lead * loads, :] = hist[0, :, block * loads:history * loads, :]
     pads[:, :half, :] = jnp.zeros((2, half, rows), F32)
 
+    inv_load.wait()
+    put(INV, inv_v[...])
     tab_hi[0:rows, :] = jnp.zeros((rows, rows), BF16)
     tab_lo[0:rows, :] = jnp.zeros((rows, rows), BF16)
 
@@ -311,8 +318,8 @@
     state_start(1)
 
     def turn_copy():
-        dst = pieces.at[c, xs_own, z]
-        return remote(tsend, dst, t_send.at[0], p_recv.at[c, z],
+        dst = pieces.at[c, xs_own, 0]
+        return remote(tsend, dst, t_send.at[0], p_recv.at[c, 0],
                       at((2 * y + nz // 2 + nz - z) % ny, x, y, x // 2))
 
     tsend[...] = outbuf[0, c, z].astype(BF16)
@@ -321,17 +328,19 @@
     def load_of(y_):
         return (2 * z + nz // 2 + nz - y_) % nz
 
-    def arrived(h, load):
-        ref = pieces.at[h, xs_own, load]
-        remote(ref, ref, t_send.at[0], p_recv.at[h, load], partner).wait_recv()
+    y_order = [0] + near_order
+
+    def arrived(h, slot):
+        ref = pieces.at[h, xs_own, slot]
+        remote(ref, ref, t_send.at[0], p_recv.at[h, slot], partner).wait_recv()
 
     def along_y(h, dy):
-        load = load_of(y)
-        ref = pieces.at[h, xs_own, load]
-        return remote(ref, ref, y_send.at[h], p_recv.at[h, load], at((y + dy) % ny, x, z, c))
-
-    def along_x(h, dy, dx):
-        ref = pieces.at[h, xs_own, load_of((y + ny - dy) % ny)]
+        slot = y_order.index(dy)
+        return remote(pieces.at[h, xs_own, 0], pieces.at[h, xs_own, slot], y_send.at[h],
+                      p_recv.at[h, slot], at((y + dy) % ny, x, z, c))
+
+    def along_x(h, first, count, dx):
+        ref = pieces.at[h, xs_own, pl.ds(first, count)]
         return remote(ref, ref, x_send.at[h, dx - 1], px_recv.at[h, xs_own],
                       at(y, (x + dx) % X, z, c))
 
@@ -348,15 +357,17 @@
     def hand_on(h):
         @pl.when(member)
         def _():
-            arrived(h, load_of(y))
+            arrived(h, 0)
             for dy in far_order:
                 along_y(h, dy).start()
-            for dx in (2, 1, 3):
-                along_x(h, 0, dx).start()
-            for dy in near_order:
-                arrived(h, load_of((y + ny - dy) % ny))
-                for dx in (2, 1, 3):
-                    along_x(h, dy, dx).start()
+            first = 0
+            for slot in range(ny):
+                if slot > 0:
+                    arrived(h, slot)
+                if slot % 2 == 1:
+                    for dx in (2, 1, 3):
+                        along_x(h, first, slot + 1 - first, dx).start()
+                    first = slot + 1
 
     def take_in(h):
         for xs in range(2):
@@ -365,9 +376,11 @@
                 all_x(h, xs, 1).wait_recv()
         for xs in range(2):
             for load in range(loads):
+                dy = (load + nz - load_of(y)) % nz
+                slot = jnp.where(dy > ny // 2, 2 * (ny - dy), jnp.maximum(2 * dy - 1, 0))
                 to = pl.ds((lead + h * half) * loads + load, half, stride=loads)
                 for k in range(rows // LANE):
-                    part_of = pieces[h, xs, load, :, k * LANE:(k + 1) * LANE]
+                    part_of = pieces[h, xs, slot, :, k * LANE:(k + 1) * LANE]
                     hist[1, xs * (rows // LANE) + k, to, :] = part_of.astype(F32)
 
     def direct_sem(blk, from_z):
@@ -529,6 +542,7 @@
             vmem((rows // LANE, hrows, LANE), F32),
             vmem((BLOCKS, nz, half, rows), F32),
             vmem((BLOCKS, nz, half, rows), F32),
+            vmem((2 * loads, rows), F32),
             vmem(((half + 1) * rows, rows), BF16),
             vmem(((half + 1) * rows, rows), BF16),
             vmem((9, rows, rows), BF16),

time: 66.6 us -> 66.8 us (level)
  Pallas kernels: 62.7 us -> 63.4 us
    pallas_call x1, Pallas kernels: 62.7 us -> 63.4 us  [local(): pl.pallas_call(functools.partial(kernel, nz=nz), out_shape=jax.ShapeDtype...]
where the time goes in v5:
time: 66.8 us; the launch traced here: 66.3 us
  Pallas kernels  63.4 us (95%)
  local copies, waits for them, and re-layouts  2.26 us (3%)
    pallas_call x1, Pallas kernels, local(): pl.pallas_call(functools.partial(kernel, nz=nz), out_shape=jax.ShapeDtype...  63.4 us
    unnamed x1, local copies, waits for them, and re-layouts  2.26 us

profile of v5, /device:TPU:1, one launch (start us, length us, event | category | flops | bytes accessed | tf_op | source)
XLA Modules:
  0.0 66.3 jit_solution(18195898772288599613)
XLA Ops:
  0.7 63.4 %shard_map.73 = f32[1024,256]{1,0:T(8,128)} custom-call(s32[12]{0:T(128)} %bitcast.5, s32[1]{0:T(128)} %bitcast.3.cnt_ref, bf16[128,8,256]{2,1,0:T(8,128)(2,1)} %inc_hbm.1, bf16[76,8,512]{2,1,0:T(8,128)(2,1)} %past_hbm.1, bf16[8,512,256]{2,1,0:T(8,128)(2,1)} %ker_hbm.1, f32[2,256,256]{2,1,0:T(8,128)} %cpl_hbm.1, f32[256,256]{1,0:T(8,128)} %inv_hbm.1), custom_call_target="tpu_custom_call" | custom-call | tf_op jit(solution)/shard_map/pallas_call | solution.py:527
  64.0 2.3 %copy.10 = f32[128,8,256]{2,1,0:T(8,128)} copy(f32[128,8,256]{2,1,0:T(8,128)} %bitcast.4) | data formatting | bytes 2097152
